TPU v7x, 256 devices: a whole 4x4x8 slice. The times are simulated.
256 devices in a mesh: wide: 32 (over y_lo, z, core), narrow: 8 (over y_hi, x).
Axes of the slice: x: 4, y: 4 (y_hi: 2, y_lo: 2; y = y_hi * 2 + y_lo), z: 8, core: 2. Of those that a mesh axis runs over, the one named last changes fastest.
Arguments:
- vectors: bfloat16 [65536, 768], P(('wide', 'narrow')), may hold values from -15 to 15
- block_sides: int32 [512], P(('wide', 'narrow')), may hold values from 0 to 1, as said below
- centers: bfloat16 [32768, 768], P(('wide', 'narrow')), may hold values from -8.5 to 8.5
Outputs:
- new_centers: bfloat16 [32768, 768], P(('wide', 'narrow'))
Inputs may be any that keep to these rules, and one draw needn't show every extreme that they name: `block_sides`: of the 2 labels of one device (consecutive runs of 2 entries), exactly half are 1.
All inputs are finite; a program needn't handle non-finite values.
Results may differ from a plain program's by a relative error of at most 0.0018.
The roundings to bfloat16 on the way count: a program that leaves them out, or rounds other values in their place, can miss the bound.
Values may be sent and summed in bfloat16 or wider, within the bound.
A program may use at most 64 MiB of HBM per device.

v0:
```python
import math
import jax
import jax.numpy as jnp
from jax import lax
from jax.sharding import PartitionSpec as P

LEVEL = 1
ITERS = 2


def from_partner(value, axis, distance):
    mask = 2**distance
    pairs = [(source, source ^ mask) for source in range(lax.axis_size(axis))]
    return lax.ppermute(value, axis, pairs)


def shifted(value, axis, steps):
    count = lax.axis_size(axis)
    pairs = [(source, (source + steps) % count) for source in range(count)]
    return lax.ppermute(value, axis, pairs)


def combined_all(part, axis, combine):
    gathered = jax.tree.map(lambda a: lax.all_gather(a, axis), part)

    def take(source):
        return jax.tree.map(lambda a: lax.dynamic_index_in_dim(a, source, 0, False), gathered)

    return lax.fori_loop(
        1, lax.axis_size(axis), lambda source, state: combine(state, take(source)), take(0)
    )


def combine_stats(first, second):
    upper = jnp.maximum(first[0], second[0])
    return (upper, first[1] * jnp.exp(first[0] - upper) + second[1] * jnp.exp(second[0] - upper))


def local(vectors, block_sides, centers):
    step_size = 2 ** (LEVEL + 1)
    cycle_len = lax.axis_size("wide") // step_size
    wide_place = lax.axis_index("wide")
    cycle_place = wide_place // step_size
    own_side = wide_place // 2**LEVEL % 2
    feat_width = vectors.shape[1]
    block_count = block_sides.shape[0]
    half_blocks = block_count // 2
    blocks = vectors.reshape(block_count, -1, feat_width)
    block_order = jnp.argsort(
        jnp.where(block_sides == own_side, 0, 1).astype(jnp.int32), stable=True
    )
    arranged = jnp.take(blocks, block_order, axis=0)
    incoming = from_partner(arranged[half_blocks:], "wide", LEVEL)
    local_rows = jnp.concatenate([arranged[:half_blocks], incoming], axis=0).reshape(-1, feat_width)
    gathered = lax.all_gather(local_rows, "narrow", axis=0, tiled=True)
    row_count = gathered.shape[0]
    shard_rows = centers.shape[0]
    score_scale = 4.0 / math.sqrt(feat_width)
    zero_index = jnp.zeros((), jnp.int32)

    def score_block(center):
        sq_norms = jnp.sum(center.astype(jnp.float32) ** 2, axis=1)
        products = lax.dot_general(
            gathered, center, (((1,), (1,)), ((), ())), preferred_element_type=jnp.float32
        )
        return score_scale * (products - 0.5 * sq_norms[None, :])

    def put_block(table, center, source):
        column = source % cycle_len * shard_rows
        return lax.dynamic_update_slice(table, score_block(center), (zero_index, column))

    def block_terms(weights, source, offset, length):
        column = source % cycle_len * shard_rows + offset
        columns = lax.dynamic_slice_in_dim(weights, column, length, 1)
        numerator = lax.dot_general(
            columns, gathered, (((0,), (0,)), ((), ())), preferred_element_type=jnp.float32
        )
        return (numerator, jnp.sum(columns.astype(jnp.float32), axis=0))

    for sweep_num in range(ITERS):
        scores = jnp.zeros((row_count, cycle_len * shard_rows), jnp.float32)
        scores = put_block(scores, centers, cycle_place)

        def stream_one(step_num, loop_state):
            current, table = loop_state
            current = shifted(current, "wide", step_size)
            return (current, put_block(table, current, cycle_place - step_num))

        current, scores = lax.fori_loop(1, cycle_len, stream_one, (centers, scores))
        row_top = jnp.max(scores, axis=1)
        row_sum = jnp.sum(jnp.exp(scores - row_top[:, None]), axis=1)
        full_top, full_sum = combined_all((row_top, row_sum), "narrow", combine_stats)
        weights = (jnp.exp(scores - full_top[:, None]) / full_sum[:, None]).astype(jnp.bfloat16)

        def gather_one(step_num, loop_state):
            moved = shifted((loop_state[0], loop_state[1]), "wide", step_size)
            added = block_terms(weights, cycle_place - step_num - 1, 0, shard_rows)
            return (moved[0] + added[0], moved[1] + added[1])

        numerator, denominator = lax.fori_loop(
            1, cycle_len, gather_one, block_terms(weights, cycle_place - 1, 0, shard_rows)
        )
        centers = ((numerator + centers.astype(jnp.float32)) / (denominator + 1.0)[:, None]).astype(
            jnp.bfloat16
        )
    return centers


def solution(mesh):
    in_specs = (P(("wide", "narrow"), None), P(("wide", "narrow")), P(("wide", "narrow"), None))
    out_specs = P(("wide", "narrow"), None)
    return jax.shard_map(local, mesh=mesh, in_specs=in_specs, out_specs=out_specs, check_vma=False)
```

profile of v0, /device:TPU:32, one launch (start us, length us, event | category | flops | bytes accessed | tf_op | source)
XLA Modules:
  0.0 849.5 jit_solution(4124487896540554424)
XLA Ops:
  10.5 4.8 collective-permute-done.6
  18.0 68.8 %all-gather.6.cloned.1.call-done = bf16[2048,768]{1,0:T(8,128)(2,1)} async-done(((bf16[256,768]{1,0:T(8,128)(2,1)}), bf16[2048,768]{1,0:T(8,128)(2,1)}) %all-gather.6.cloned.1.call-update) | async-done | bytes 3145744 | tf_op jit(solution)/shard_map/all_gather | solution.py:55
  92.8 114.8 %while.102 = (s32[]{:T(128)}, bf16[128,768]{1,0:T(8,128)(2,1)}, f32[2048,1024]{1,0:T(8,128)}, bf16[2048,768]{1,0:T(8,128)(2,1)S(1)}, s32[]{:T(128)}, /*index=5*/...) while((s32[]{:T(128)}, bf16[128,768]{1,0:T(8,128)(2,1)}, ...), condition=%wide.region_4.5_spmd, body=%wide.region_2.4_spmd.sunk | while | flops 403472416 | bytes 5769536 | solution.py:89
  95.4 10.8 %collective-permute-done = bf16[128,768]{1,0:T(8,128)(2,1)} collective-permute-done((bf16[128,768]{1,0:T(8,128)(2,1)}, bf16[128,768]{1,0:T(8,128)(2,1)}, u32[]{:S(2)}, u32[]{:S(2)}) %collective-permute-start) | collective-permute-done | bytes 196640 | tf_op jit(solution)/shard_map/while/body/eval_jaxpr/ppermute | solution.py:20
  112.4 12.0 %collective-permute-done = bf16[128,768]{1,0:T(8,128)(2,1)} collective-permute-done((bf16[128,768]{1,0:T(8,128)(2,1)}, bf16[128,768]{1,0:T(8,128)(2,1)}, u32[]{:S(2)}, u32[]{:S(2)}) %collective-permute-start) | collective-permute-done | bytes 196640 | tf_op jit(solution)/shard_map/while/body/eval_jaxpr/ppermute | solution.py:20
  130.0 12.0 %collective-permute-done = bf16[128,768]{1,0:T(8,128)(2,1)} collective-permute-done((bf16[128,768]{1,0:T(8,128)(2,1)}, bf16[128,768]{1,0:T(8,128)(2,1)}, u32[]{:S(2)}, u32[]{:S(2)}) %collective-permute-start) | collective-permute-done | bytes 196640 | tf_op jit(solution)/shard_map/while/body/eval_jaxpr/ppermute | solution.py:20
  147.6 9.2 %collective-permute-done = bf16[128,768]{1,0:T(8,128)(2,1)} collective-permute-done((bf16[128,768]{1,0:T(8,128)(2,1)}, bf16[128,768]{1,0:T(8,128)(2,1)}, u32[]{:S(2)}, u32[]{:S(2)}) %collective-permute-start) | collective-permute-done | bytes 196640 | tf_op jit(solution)/shard_map/while/body/eval_jaxpr/ppermute | solution.py:20
  162.4 9.1 %collective-permute-done = bf16[128,768]{1,0:T(8,128)(2,1)} collective-permute-done((bf16[128,768]{1,0:T(8,128)(2,1)}, bf16[128,768]{1,0:T(8,128)(2,1)}, u32[]{:S(2)}, u32[]{:S(2)}) %collective-permute-start) | collective-permute-done | bytes 196640 | tf_op jit(solution)/shard_map/while/body/eval_jaxpr/ppermute | solution.py:20
  177.2 10.0 %collective-permute-done = bf16[128,768]{1,0:T(8,128)(2,1)} collective-permute-done((bf16[128,768]{1,0:T(8,128)(2,1)}, bf16[128,768]{1,0:T(8,128)(2,1)}, u32[]{:S(2)}, u32[]{:S(2)}) %collective-permute-start) | collective-permute-done | bytes 196640 | tf_op jit(solution)/shard_map/while/body/eval_jaxpr/ppermute | solution.py:20
  192.8 9.2 %collective-permute-done = bf16[128,768]{1,0:T(8,128)(2,1)} collective-permute-done((bf16[128,768]{1,0:T(8,128)(2,1)}, bf16[128,768]{1,0:T(8,128)(2,1)}, u32[]{:S(2)}, u32[]{:S(2)}) %collective-permute-start) | collective-permute-done | bytes 196640 | tf_op jit(solution)/shard_map/while/body/eval_jaxpr/ppermute | solution.py:20
  215.8 36.2 %all-gather.1 = f32[16384]{0:T(1024)} all-gather(f32[2048]{0:T(1024)S(1)} %exponential_reduce_fusion.1), channel_id=3, replica_groups=mesh['wide'=32,'narrow'=8] {'narrow'}, dimensions={0}, use_global_device_ids=true | all-gather | bytes 73728 | tf_op jit(solution)/shard_map/all_gather | solution.py:24
  254.2 36.3 %all-gather = f32[16384]{0:T(1024)} all-gather(f32[2048]{0:T(1024)S(1)} %reduce_max.18), channel_id=2, replica_groups=mesh['wide'=32,'narrow'=8] {'narrow'}, dimensions={0}, use_global_device_ids=true | all-gather | bytes 73728 | tf_op jit(solution)/shard_map/all_gather | solution.py:24
  292.7 6.5 while.103
  305.5 155.7 %while.104 = (s32[]{:T(128)}, f32[128,768]{1,0:T(8,128)}, f32[128]{0:T(128)S(1)}, s32[]{:T(128)}, bf16[2048,1024]{1,0:T(8,128)(2,1)}, /*index=5*/bf16[2048,768]{...) while((s32[]{:T(128)}, f32[128,768]{1,0:T(8,128)}, ...), condition=%wide.region_12.13_spmd, body=%wide.region_10.12_spmd.sunk | while | flops 403275808 | bytes 6558088 | solution.py:100
  307.0 4.7 collective-permute-start.2
  313.0 12.6 %collective-permute-done.2 = f32[128]{0:T(128)S(1)} collective-permute-done((f32[128]{0:T(128)S(1)}, f32[128]{0:T(128)S(1)}, u32[]{:S(2)}, u32[]{:S(2)}) %collective-permute-start.2) | collective-permute-done | bytes 544 | tf_op jit(solution)/shard_map/while/body/eval_jaxpr/ppermute | solution.py:20
  330.7 7.3 collective-permute-start.2
  339.3 9.2 %collective-permute-done.2 = f32[128]{0:T(128)S(1)} collective-permute-done((f32[128]{0:T(128)S(1)}, f32[128]{0:T(128)S(1)}, u32[]{:S(2)}, u32[]{:S(2)}) %collective-permute-start.2) | collective-permute-done | bytes 544 | tf_op jit(solution)/shard_map/while/body/eval_jaxpr/ppermute | solution.py:20
  351.0 7.3 collective-permute-start.1
  358.3 4.6 collective-permute-start.2
  364.2 8.9 %collective-permute-done.2 = f32[128]{0:T(128)S(1)} collective-permute-done((f32[128]{0:T(128)S(1)}, f32[128]{0:T(128)S(1)}, u32[]{:S(2)}, u32[]{:S(2)}) %collective-permute-start.2) | collective-permute-done | bytes 544 | tf_op jit(solution)/shard_map/while/body/eval_jaxpr/ppermute | solution.py:20
  380.0 4.6 collective-permute-start.2
  385.8 7.8 collective-permute-done.2
  404.2 12.3 %collective-permute-done.2 = f32[128]{0:T(128)S(1)} collective-permute-done((f32[128]{0:T(128)S(1)}, f32[128]{0:T(128)S(1)}, u32[]{:S(2)}, u32[]{:S(2)}) %collective-permute-start.2) | collective-permute-done | bytes 544 | tf_op jit(solution)/shard_map/while/body/eval_jaxpr/ppermute | solution.py:20
  425.5 13.0 %collective-permute-done.2 = f32[128]{0:T(128)S(1)} collective-permute-done((f32[128]{0:T(128)S(1)}, f32[128]{0:T(128)S(1)}, u32[]{:S(2)}, u32[]{:S(2)}) %collective-permute-start.2) | collective-permute-done | bytes 544 | tf_op jit(solution)/shard_map/while/body/eval_jaxpr/ppermute | solution.py:20
  444.5 5.8 collective-permute-start.2
  451.6 7.0 collective-permute-done.2
  468.4 115.8 %while.105 = (s32[]{:T(128)}, bf16[128,768]{1,0:T(8,128)(2,1)}, f32[2048,1024]{1,0:T(8,128)}, bf16[2048,768]{1,0:T(8,128)(2,1)S(1)}, s32[]{:T(128)}, /*index=5*/...) while((s32[]{:T(128)}, bf16[128,768]{1,0:T(8,128)(2,1)}, ...), condition=%wide.region_16.17_spmd, body=%wide.region_14.16_spmd.sunk | while | flops 403472416 | bytes 5769536 | solution.py:89
  472.7 7.4 collective-permute-done.3
  488.5 6.9 collective-permute-done.3
  504.3 5.8 collective-permute-done.3
  530.4 7.6 collective-permute-start.3
  537.9 5.5 collective-permute-done.3
  549.1 5.9 collective-permute-start.3
  564.1 9.0 %collective-permute-start.3 = (bf16[128,768]{1,0:T(8,128)(2,1)}, bf16[128,768]{1,0:T(8,128)(2,1)}, u32[]{:S(2)}, u32[]{:S(2)}) collective-permute-start(bf16[128,768]{1,0:T(8,128)(2,1)} %get-tuple-element.1261), channel_id=1, source_target_pairs={{0,32},{8,40},{16,48},{24,56},{32,64},{40,72},{48,80},{56,88},{64,... | collective-permute-start | bytes 589832 | tf_op jit(solution)/shard_map/while/body/eval_jaxpr/ppermute | solution.py:20
  573.0 5.6 collective-permute-done.3
  592.5 46.8 %all-gather.3 = f32[16384]{0:T(1024)} all-gather(f32[2048]{0:T(1024)S(1)} %exponential_reduce_fusion), channel_id=5, replica_groups=mesh['wide'=32,'narrow'=8] {'narrow'}, dimensions={0}, use_global_device_ids=true | all-gather | bytes 73728 | tf_op jit(solution)/shard_map/all_gather | solution.py:24
  641.5 36.4 %all-gather.2 = f32[16384]{0:T(1024)} all-gather(f32[2048]{0:T(1024)S(1)} %reduce_max.19), channel_id=4, replica_groups=mesh['wide'=32,'narrow'=8] {'narrow'}, dimensions={0}, use_global_device_ids=true | all-gather | bytes 73728 | tf_op jit(solution)/shard_map/all_gather | solution.py:24
  680.0 6.5 while.106
  692.9 147.9 %while.107 = (s32[]{:T(128)}, f32[128,768]{1,0:T(8,128)}, f32[128]{0:T(128)S(1)}, s32[]{:T(128)}, bf16[2048,1024]{1,0:T(8,128)(2,1)}, /*index=5*/bf16[2048,768]{...) while((s32[]{:T(128)}, f32[128,768]{1,0:T(8,128)}, ...), condition=%wide.region_24.25_spmd, body=%wide.region_22.24_spmd.sunk | while | flops 403275808 | bytes 6558088 | solution.py:100
  696.9 4.6 collective-permute-start.5
  702.8 13.7 %collective-permute-done.5 = f32[128]{0:T(128)S(1)} collective-permute-done((f32[128]{0:T(128)S(1)}, f32[128]{0:T(128)S(1)}, u32[]{:S(2)}, u32[]{:S(2)}) %collective-permute-start.5) | collective-permute-done | bytes 544 | tf_op jit(solution)/shard_map/while/body/eval_jaxpr/ppermute | solution.py:20
  720.4 19.4 %collective-permute-done.5 = f32[128]{0:T(128)S(1)} collective-permute-done((f32[128]{0:T(128)S(1)}, f32[128]{0:T(128)S(1)}, u32[]{:S(2)}, u32[]{:S(2)}) %collective-permute-start.5) | collective-permute-done | bytes 544 | tf_op jit(solution)/shard_map/while/body/eval_jaxpr/ppermute | solution.py:20
  743.7 21.9 %collective-permute-done.5 = f32[128]{0:T(128)S(1)} collective-permute-done((f32[128]{0:T(128)S(1)}, f32[128]{0:T(128)S(1)}, u32[]{:S(2)}, u32[]{:S(2)}) %collective-permute-start.5) | collective-permute-done | bytes 544 | tf_op jit(solution)/shard_map/while/body/eval_jaxpr/ppermute | solution.py:20
  769.6 18.2 %collective-permute-done.5 = f32[128]{0:T(128)S(1)} collective-permute-done((f32[128]{0:T(128)S(1)}, f32[128]{0:T(128)S(1)}, u32[]{:S(2)}, u32[]{:S(2)}) %collective-permute-start.5) | collective-permute-done | bytes 544 | tf_op jit(solution)/shard_map/while/body/eval_jaxpr/ppermute | solution.py:20
  791.7 11.0 %collective-permute-done.5 = f32[128]{0:T(128)S(1)} collective-permute-done((f32[128]{0:T(128)S(1)}, f32[128]{0:T(128)S(1)}, u32[]{:S(2)}, u32[]{:S(2)}) %collective-permute-start.5) | collective-permute-done | bytes 544 | tf_op jit(solution)/shard_map/while/body/eval_jaxpr/ppermute | solution.py:20
  806.5 14.0 %collective-permute-done.5 = f32[128]{0:T(128)S(1)} collective-permute-done((f32[128]{0:T(128)S(1)}, f32[128]{0:T(128)S(1)}, u32[]{:S(2)}, u32[]{:S(2)}) %collective-permute-start.5) | collective-permute-done | bytes 544 | tf_op jit(solution)/shard_map/while/body/eval_jaxpr/ppermute | solution.py:20
  824.3 13.9 %collective-permute-done.5 = f32[128]{0:T(128)S(1)} collective-permute-done((f32[128]{0:T(128)S(1)}, f32[128]{0:T(128)S(1)}, u32[]{:S(2)}, u32[]{:S(2)}) %collective-permute-start.5) | collective-permute-done | bytes 544 | tf_op jit(solution)/shard_map/while/body/eval_jaxpr/ppermute | solution.py:20
  (236 shorter events, 258.5 us)
Async XLA Ops:
  6.5 11.3 %copy-start.6 = (bf16[128,768]{1,0:T(8,128)(2,1)S(1)}, bf16[128,768]{1,0:T(8,128)(2,1)}, u32[]{:S(2)}) copy-start(bf16[128,768]{1,0:T(8,128)(2,1)} %param.17) | copy-start | bytes 589828
  6.5 80.2 %all-gather.6.cloned.1.call-start = ((), (), s32[]{:S(2)}) async-start(), calls=%async_computation | async-start | bytes 3538944 | tf_op jit(solution)/shard_map/all_gather | solution.py:55
  8.6 6.7 collective-permute-start.6
  89.6 3.2 copy-start.3
  92.8 13.4 %collective-permute-start = (bf16[128,768]{1,0:T(8,128)(2,1)}, bf16[128,768]{1,0:T(8,128)(2,1)}, u32[]{:S(2)}, u32[]{:S(2)}) collective-permute-start(bf16[128,768]{1,0:T(8,128)(2,1)} %get-tuple-element.1165), channel_id=1, source_target_pairs={{0,32},{8,40},{16,48},{24,56},{32,64},{40,72},{48,80},{56,88},{64,... | collective-permute-start | bytes 589832 | tf_op jit(solution)/shard_map/while/body/eval_jaxpr/ppermute | solution.py:20
  111.8 12.6 %collective-permute-start = (bf16[128,768]{1,0:T(8,128)(2,1)}, bf16[128,768]{1,0:T(8,128)(2,1)}, u32[]{:S(2)}, u32[]{:S(2)}) collective-permute-start(bf16[128,768]{1,0:T(8,128)(2,1)} %get-tuple-element.1165), channel_id=1, source_target_pairs={{0,32},{8,40},{16,48},{24,56},{32,64},{40,72},{48,80},{56,88},{64,... | collective-permute-start | bytes 589832 | tf_op jit(solution)/shard_map/while/body/eval_jaxpr/ppermute | solution.py:20
  130.0 12.0 %collective-permute-start = (bf16[128,768]{1,0:T(8,128)(2,1)}, bf16[128,768]{1,0:T(8,128)(2,1)}, u32[]{:S(2)}, u32[]{:S(2)}) collective-permute-start(bf16[128,768]{1,0:T(8,128)(2,1)} %get-tuple-element.1165), channel_id=1, source_target_pairs={{0,32},{8,40},{16,48},{24,56},{32,64},{40,72},{48,80},{56,88},{64,... | collective-permute-start | bytes 589832 | tf_op jit(solution)/shard_map/while/body/eval_jaxpr/ppermute | solution.py:20
  147.6 9.2 %collective-permute-start = (bf16[128,768]{1,0:T(8,128)(2,1)}, bf16[128,768]{1,0:T(8,128)(2,1)}, u32[]{:S(2)}, u32[]{:S(2)}) collective-permute-start(bf16[128,768]{1,0:T(8,128)(2,1)} %get-tuple-element.1165), channel_id=1, source_target_pairs={{0,32},{8,40},{16,48},{24,56},{32,64},{40,72},{48,80},{56,88},{64,... | collective-permute-start | bytes 589832 | tf_op jit(solution)/shard_map/while/body/eval_jaxpr/ppermute | solution.py:20
  162.4 9.1 %collective-permute-start = (bf16[128,768]{1,0:T(8,128)(2,1)}, bf16[128,768]{1,0:T(8,128)(2,1)}, u32[]{:S(2)}, u32[]{:S(2)}) collective-permute-start(bf16[128,768]{1,0:T(8,128)(2,1)} %get-tuple-element.1165), channel_id=1, source_target_pairs={{0,32},{8,40},{16,48},{24,56},{32,64},{40,72},{48,80},{56,88},{64,... | collective-permute-start | bytes 589832 | tf_op jit(solution)/shard_map/while/body/eval_jaxpr/ppermute | solution.py:20
  177.2 10.0 %collective-permute-start = (bf16[128,768]{1,0:T(8,128)(2,1)}, bf16[128,768]{1,0:T(8,128)(2,1)}, u32[]{:S(2)}, u32[]{:S(2)}) collective-permute-start(bf16[128,768]{1,0:T(8,128)(2,1)} %get-tuple-element.1165), channel_id=1, source_target_pairs={{0,32},{8,40},{16,48},{24,56},{32,64},{40,72},{48,80},{56,88},{64,... | collective-permute-start | bytes 589832 | tf_op jit(solution)/shard_map/while/body/eval_jaxpr/ppermute | solution.py:20
  192.8 9.2 %collective-permute-start = (bf16[128,768]{1,0:T(8,128)(2,1)}, bf16[128,768]{1,0:T(8,128)(2,1)}, u32[]{:S(2)}, u32[]{:S(2)}) collective-permute-start(bf16[128,768]{1,0:T(8,128)(2,1)} %get-tuple-element.1165), channel_id=1, source_target_pairs={{0,32},{8,40},{16,48},{24,56},{32,64},{40,72},{48,80},{56,88},{64,... | collective-permute-start | bytes 589832 | tf_op jit(solution)/shard_map/while/body/eval_jaxpr/ppermute | solution.py:20
  303.4 2.1 copy-start.5
  305.5 20.1 %collective-permute-start.1 = (f32[128,768]{1,0:T(8,128)}, f32[128,768]{1,0:T(8,128)}, u32[]{:S(2)}, u32[]{:S(2)}) collective-permute-start(f32[128,768]{1,0:T(8,128)} %get-tuple-element.1224), channel_id=1, source_target_pairs={{0,32},{8,40},{16,48},{24,56},{32,64},{40,72},{48,80},{56,88},{64,... | collective-permute-start | bytes 1179656 | tf_op jit(solution)/shard_map/while/body/eval_jaxpr/ppermute | solution.py:20
  307.0 18.6 %collective-permute-start.2 = (f32[128]{0:T(128)S(1)}, f32[128]{0:T(128)S(1)}, u32[]{:S(2)}, u32[]{:S(2)}) collective-permute-start(f32[128]{0:T(128)S(1)} %get-tuple-element.1225), channel_id=1, source_target_pairs={{0,32},{8,40},{16,48},{24,56},{32,64},{40,72},{48,80},{56,88},{64,... | collective-permute-start | bytes 1544 | tf_op jit(solution)/shard_map/while/body/eval_jaxpr/ppermute | solution.py:20
  328.1 20.3 %collective-permute-start.1 = (f32[128,768]{1,0:T(8,128)}, f32[128,768]{1,0:T(8,128)}, u32[]{:S(2)}, u32[]{:S(2)}) collective-permute-start(f32[128,768]{1,0:T(8,128)} %get-tuple-element.1224), channel_id=1, source_target_pairs={{0,32},{8,40},{16,48},{24,56},{32,64},{40,72},{48,80},{56,88},{64,... | collective-permute-start | bytes 1179656 | tf_op jit(solution)/shard_map/while/body/eval_jaxpr/ppermute | solution.py:20
  330.7 17.8 %collective-permute-start.2 = (f32[128]{0:T(128)S(1)}, f32[128]{0:T(128)S(1)}, u32[]{:S(2)}, u32[]{:S(2)}) collective-permute-start(f32[128]{0:T(128)S(1)} %get-tuple-element.1225), channel_id=1, source_target_pairs={{0,32},{8,40},{16,48},{24,56},{32,64},{40,72},{48,80},{56,88},{64,... | collective-permute-start | bytes 1544 | tf_op jit(solution)/shard_map/while/body/eval_jaxpr/ppermute | solution.py:20
  351.0 22.1 %collective-permute-start.1 = (f32[128,768]{1,0:T(8,128)}, f32[128,768]{1,0:T(8,128)}, u32[]{:S(2)}, u32[]{:S(2)}) collective-permute-start(f32[128,768]{1,0:T(8,128)} %get-tuple-element.1224), channel_id=1, source_target_pairs={{0,32},{8,40},{16,48},{24,56},{32,64},{40,72},{48,80},{56,88},{64,... | collective-permute-start | bytes 1179656 | tf_op jit(solution)/shard_map/while/body/eval_jaxpr/ppermute | solution.py:20
  358.3 14.8 %collective-permute-start.2 = (f32[128]{0:T(128)S(1)}, f32[128]{0:T(128)S(1)}, u32[]{:S(2)}, u32[]{:S(2)}) collective-permute-start(f32[128]{0:T(128)S(1)} %get-tuple-element.1225), channel_id=1, source_target_pairs={{0,32},{8,40},{16,48},{24,56},{32,64},{40,72},{48,80},{56,88},{64,... | collective-permute-start | bytes 1544 | tf_op jit(solution)/shard_map/while/body/eval_jaxpr/ppermute | solution.py:20
  375.6 18.0 %collective-permute-start.1 = (f32[128,768]{1,0:T(8,128)}, f32[128,768]{1,0:T(8,128)}, u32[]{:S(2)}, u32[]{:S(2)}) collective-permute-start(f32[128,768]{1,0:T(8,128)} %get-tuple-element.1224), channel_id=1, source_target_pairs={{0,32},{8,40},{16,48},{24,56},{32,64},{40,72},{48,80},{56,88},{64,... | collective-permute-start | bytes 1179656 | tf_op jit(solution)/shard_map/while/body/eval_jaxpr/ppermute | solution.py:20
  380.0 13.7 %collective-permute-start.2 = (f32[128]{0:T(128)S(1)}, f32[128]{0:T(128)S(1)}, u32[]{:S(2)}, u32[]{:S(2)}) collective-permute-start(f32[128]{0:T(128)S(1)} %get-tuple-element.1225), channel_id=1, source_target_pairs={{0,32},{8,40},{16,48},{24,56},{32,64},{40,72},{48,80},{56,88},{64,... | collective-permute-start | bytes 1544 | tf_op jit(solution)/shard_map/while/body/eval_jaxpr/ppermute | solution.py:20
  396.2 20.4 %collective-permute-start.1 = (f32[128,768]{1,0:T(8,128)}, f32[128,768]{1,0:T(8,128)}, u32[]{:S(2)}, u32[]{:S(2)}) collective-permute-start(f32[128,768]{1,0:T(8,128)} %get-tuple-element.1224), channel_id=1, source_target_pairs={{0,32},{8,40},{16,48},{24,56},{32,64},{40,72},{48,80},{56,88},{64,... | collective-permute-start | bytes 1179656 | tf_op jit(solution)/shard_map/while/body/eval_jaxpr/ppermute | solution.py:20
  399.6 16.9 %collective-permute-start.2 = (f32[128]{0:T(128)S(1)}, f32[128]{0:T(128)S(1)}, u32[]{:S(2)}, u32[]{:S(2)}) collective-permute-start(f32[128]{0:T(128)S(1)} %get-tuple-element.1225), channel_id=1, source_target_pairs={{0,32},{8,40},{16,48},{24,56},{32,64},{40,72},{48,80},{56,88},{64,... | collective-permute-start | bytes 1544 | tf_op jit(solution)/shard_map/while/body/eval_jaxpr/ppermute | solution.py:20
  419.1 19.5 %collective-permute-start.1 = (f32[128,768]{1,0:T(8,128)}, f32[128,768]{1,0:T(8,128)}, u32[]{:S(2)}, u32[]{:S(2)}) collective-permute-start(f32[128,768]{1,0:T(8,128)} %get-tuple-element.1224), channel_id=1, source_target_pairs={{0,32},{8,40},{16,48},{24,56},{32,64},{40,72},{48,80},{56,88},{64,... | collective-permute-start | bytes 1179656 | tf_op jit(solution)/shard_map/while/body/eval_jaxpr/ppermute | solution.py:20
  422.4 16.1 %collective-permute-start.2 = (f32[128]{0:T(128)S(1)}, f32[128]{0:T(128)S(1)}, u32[]{:S(2)}, u32[]{:S(2)}) collective-permute-start(f32[128]{0:T(128)S(1)} %get-tuple-element.1225), channel_id=1, source_target_pairs={{0,32},{8,40},{16,48},{24,56},{32,64},{40,72},{48,80},{56,88},{64,... | collective-permute-start | bytes 1544 | tf_op jit(solution)/shard_map/while/body/eval_jaxpr/ppermute | solution.py:20
  441.1 17.5 %collective-permute-start.1 = (f32[128,768]{1,0:T(8,128)}, f32[128,768]{1,0:T(8,128)}, u32[]{:S(2)}, u32[]{:S(2)}) collective-permute-start(f32[128,768]{1,0:T(8,128)} %get-tuple-element.1224), channel_id=1, source_target_pairs={{0,32},{8,40},{16,48},{24,56},{32,64},{40,72},{48,80},{56,88},{64,... | collective-permute-start | bytes 1179656 | tf_op jit(solution)/shard_map/while/body/eval_jaxpr/ppermute | solution.py:20
  444.5 14.1 %collective-permute-start.2 = (f32[128]{0:T(128)S(1)}, f32[128]{0:T(128)S(1)}, u32[]{:S(2)}, u32[]{:S(2)}) collective-permute-start(f32[128]{0:T(128)S(1)} %get-tuple-element.1225), channel_id=1, source_target_pairs={{0,32},{8,40},{16,48},{24,56},{32,64},{40,72},{48,80},{56,88},{64,... | collective-permute-start | bytes 1544 | tf_op jit(solution)/shard_map/while/body/eval_jaxpr/ppermute | solution.py:20
  465.2 3.2 copy-start.2
  468.4 11.7 %collective-permute-start.3 = (bf16[128,768]{1,0:T(8,128)(2,1)}, bf16[128,768]{1,0:T(8,128)(2,1)}, u32[]{:S(2)}, u32[]{:S(2)}) collective-permute-start(bf16[128,768]{1,0:T(8,128)(2,1)} %get-tuple-element.1261), channel_id=1, source_target_pairs={{0,32},{8,40},{16,48},{24,56},{32,64},{40,72},{48,80},{56,88},{64,... | collective-permute-start | bytes 589832 | tf_op jit(solution)/shard_map/while/body/eval_jaxpr/ppermute | solution.py:20
  485.8 9.6 %collective-permute-start.3 = (bf16[128,768]{1,0:T(8,128)(2,1)}, bf16[128,768]{1,0:T(8,128)(2,1)}, u32[]{:S(2)}, u32[]{:S(2)}) collective-permute-start(bf16[128,768]{1,0:T(8,128)(2,1)} %get-tuple-element.1261), channel_id=1, source_target_pairs={{0,32},{8,40},{16,48},{24,56},{32,64},{40,72},{48,80},{56,88},{64,... | collective-permute-start | bytes 589832 | tf_op jit(solution)/shard_map/while/body/eval_jaxpr/ppermute | solution.py:20
  501.0 9.1 %collective-permute-start.3 = (bf16[128,768]{1,0:T(8,128)(2,1)}, bf16[128,768]{1,0:T(8,128)(2,1)}, u32[]{:S(2)}, u32[]{:S(2)}) collective-permute-start(bf16[128,768]{1,0:T(8,128)(2,1)} %get-tuple-element.1261), channel_id=1, source_target_pairs={{0,32},{8,40},{16,48},{24,56},{32,64},{40,72},{48,80},{56,88},{64,... | collective-permute-start | bytes 589832 | tf_op jit(solution)/shard_map/while/body/eval_jaxpr/ppermute | solution.py:20
  515.8 9.0 %collective-permute-start.3 = (bf16[128,768]{1,0:T(8,128)(2,1)}, bf16[128,768]{1,0:T(8,128)(2,1)}, u32[]{:S(2)}, u32[]{:S(2)}) collective-permute-start(bf16[128,768]{1,0:T(8,128)(2,1)} %get-tuple-element.1261), channel_id=1, source_target_pairs={{0,32},{8,40},{16,48},{24,56},{32,64},{40,72},{48,80},{56,88},{64,... | collective-permute-start | bytes 589832 | tf_op jit(solution)/shard_map/while/body/eval_jaxpr/ppermute | solution.py:20
  530.4 13.1 %collective-permute-start.3 = (bf16[128,768]{1,0:T(8,128)(2,1)}, bf16[128,768]{1,0:T(8,128)(2,1)}, u32[]{:S(2)}, u32[]{:S(2)}) collective-permute-start(bf16[128,768]{1,0:T(8,128)(2,1)} %get-tuple-element.1261), channel_id=1, source_target_pairs={{0,32},{8,40},{16,48},{24,56},{32,64},{40,72},{48,80},{56,88},{64,... | collective-permute-start | bytes 589832 | tf_op jit(solution)/shard_map/while/body/eval_jaxpr/ppermute | solution.py:20
  549.1 9.4 %collective-permute-start.3 = (bf16[128,768]{1,0:T(8,128)(2,1)}, bf16[128,768]{1,0:T(8,128)(2,1)}, u32[]{:S(2)}, u32[]{:S(2)}) collective-permute-start(bf16[128,768]{1,0:T(8,128)(2,1)} %get-tuple-element.1261), channel_id=1, source_target_pairs={{0,32},{8,40},{16,48},{24,56},{32,64},{40,72},{48,80},{56,88},{64,... | collective-permute-start | bytes 589832 | tf_op jit(solution)/shard_map/while/body/eval_jaxpr/ppermute | solution.py:20
  564.1 14.5 %collective-permute-start.3 = (bf16[128,768]{1,0:T(8,128)(2,1)}, bf16[128,768]{1,0:T(8,128)(2,1)}, u32[]{:S(2)}, u32[]{:S(2)}) collective-permute-start(bf16[128,768]{1,0:T(8,128)(2,1)} %get-tuple-element.1261), channel_id=1, source_target_pairs={{0,32},{8,40},{16,48},{24,56},{32,64},{40,72},{48,80},{56,88},{64,... | collective-permute-start | bytes 589832 | tf_op jit(solution)/shard_map/while/body/eval_jaxpr/ppermute | solution.py:20
  692.9 23.7 %collective-permute-start.4 = (f32[128,768]{1,0:T(8,128)}, f32[128,768]{1,0:T(8,128)}, u32[]{:S(2)}, u32[]{:S(2)}) collective-permute-start(f32[128,768]{1,0:T(8,128)} %get-tuple-element.1320), channel_id=1, source_target_pairs={{0,32},{8,40},{16,48},{24,56},{32,64},{40,72},{48,80},{56,88},{64,... | collective-permute-start | bytes 1179656 | tf_op jit(solution)/shard_map/while/body/eval_jaxpr/ppermute | solution.py:20
  696.9 19.6 %collective-permute-start.5 = (f32[128]{0:T(128)S(1)}, f32[128]{0:T(128)S(1)}, u32[]{:S(2)}, u32[]{:S(2)}) collective-permute-start(f32[128]{0:T(128)S(1)} %get-tuple-element.1321), channel_id=1, source_target_pairs={{0,32},{8,40},{16,48},{24,56},{32,64},{40,72},{48,80},{56,88},{64,... | collective-permute-start | bytes 1544 | tf_op jit(solution)/shard_map/while/body/eval_jaxpr/ppermute | solution.py:20
  719.1 20.8 %collective-permute-start.4 = (f32[128,768]{1,0:T(8,128)}, f32[128,768]{1,0:T(8,128)}, u32[]{:S(2)}, u32[]{:S(2)}) collective-permute-start(f32[128,768]{1,0:T(8,128)} %get-tuple-element.1320), channel_id=1, source_target_pairs={{0,32},{8,40},{16,48},{24,56},{32,64},{40,72},{48,80},{56,88},{64,... | collective-permute-start | bytes 1179656 | tf_op jit(solution)/shard_map/while/body/eval_jaxpr/ppermute | solution.py:20
  719.1 20.8 %collective-permute-start.5 = (f32[128]{0:T(128)S(1)}, f32[128]{0:T(128)S(1)}, u32[]{:S(2)}, u32[]{:S(2)}) collective-permute-start(f32[128]{0:T(128)S(1)} %get-tuple-element.1321), channel_id=1, source_target_pairs={{0,32},{8,40},{16,48},{24,56},{32,64},{40,72},{48,80},{56,88},{64,... | collective-permute-start | bytes 1544 | tf_op jit(solution)/shard_map/while/body/eval_jaxpr/ppermute | solution.py:20
  742.4 23.3 %collective-permute-start.4 = (f32[128,768]{1,0:T(8,128)}, f32[128,768]{1,0:T(8,128)}, u32[]{:S(2)}, u32[]{:S(2)}) collective-permute-start(f32[128,768]{1,0:T(8,128)} %get-tuple-element.1320), channel_id=1, source_target_pairs={{0,32},{8,40},{16,48},{24,56},{32,64},{40,72},{48,80},{56,88},{64,... | collective-permute-start | bytes 1179656 | tf_op jit(solution)/shard_map/while/body/eval_jaxpr/ppermute | solution.py:20
  742.4 23.3 %collective-permute-start.5 = (f32[128]{0:T(128)S(1)}, f32[128]{0:T(128)S(1)}, u32[]{:S(2)}, u32[]{:S(2)}) collective-permute-start(f32[128]{0:T(128)S(1)} %get-tuple-element.1321), channel_id=1, source_target_pairs={{0,32},{8,40},{16,48},{24,56},{32,64},{40,72},{48,80},{56,88},{64,... | collective-permute-start | bytes 1544 | tf_op jit(solution)/shard_map/while/body/eval_jaxpr/ppermute | solution.py:20
  768.2 19.6 %collective-permute-start.4 = (f32[128,768]{1,0:T(8,128)}, f32[128,768]{1,0:T(8,128)}, u32[]{:S(2)}, u32[]{:S(2)}) collective-permute-start(f32[128,768]{1,0:T(8,128)} %get-tuple-element.1320), channel_id=1, source_target_pairs={{0,32},{8,40},{16,48},{24,56},{32,64},{40,72},{48,80},{56,88},{64,... | collective-permute-start | bytes 1179656 | tf_op jit(solution)/shard_map/while/body/eval_jaxpr/ppermute | solution.py:20
  768.2 19.5 %collective-permute-start.5 = (f32[128]{0:T(128)S(1)}, f32[128]{0:T(128)S(1)}, u32[]{:S(2)}, u32[]{:S(2)}) collective-permute-start(f32[128]{0:T(128)S(1)} %get-tuple-element.1321), channel_id=1, source_target_pairs={{0,32},{8,40},{16,48},{24,56},{32,64},{40,72},{48,80},{56,88},{64,... | collective-permute-start | bytes 1544 | tf_op jit(solution)/shard_map/while/body/eval_jaxpr/ppermute | solution.py:20
  790.3 12.3 %collective-permute-start.4 = (f32[128,768]{1,0:T(8,128)}, f32[128,768]{1,0:T(8,128)}, u32[]{:S(2)}, u32[]{:S(2)}) collective-permute-start(f32[128,768]{1,0:T(8,128)} %get-tuple-element.1320), channel_id=1, source_target_pairs={{0,32},{8,40},{16,48},{24,56},{32,64},{40,72},{48,80},{56,88},{64,... | collective-permute-start | bytes 1179656 | tf_op jit(solution)/shard_map/while/body/eval_jaxpr/ppermute | solution.py:20
  790.3 12.3 %collective-permute-start.5 = (f32[128]{0:T(128)S(1)}, f32[128]{0:T(128)S(1)}, u32[]{:S(2)}, u32[]{:S(2)}) collective-permute-start(f32[128]{0:T(128)S(1)} %get-tuple-element.1321), channel_id=1, source_target_pairs={{0,32},{8,40},{16,48},{24,56},{32,64},{40,72},{48,80},{56,88},{64,... | collective-permute-start | bytes 1544 | tf_op jit(solution)/shard_map/while/body/eval_jaxpr/ppermute | solution.py:20
  805.2 15.3 %collective-permute-start.4 = (f32[128,768]{1,0:T(8,128)}, f32[128,768]{1,0:T(8,128)}, u32[]{:S(2)}, u32[]{:S(2)}) collective-permute-start(f32[128,768]{1,0:T(8,128)} %get-tuple-element.1320), channel_id=1, source_target_pairs={{0,32},{8,40},{16,48},{24,56},{32,64},{40,72},{48,80},{56,88},{64,... | collective-permute-start | bytes 1179656 | tf_op jit(solution)/shard_map/while/body/eval_jaxpr/ppermute | solution.py:20
  805.2 15.3 %collective-permute-start.5 = (f32[128]{0:T(128)S(1)}, f32[128]{0:T(128)S(1)}, u32[]{:S(2)}, u32[]{:S(2)}) collective-permute-start(f32[128]{0:T(128)S(1)} %get-tuple-element.1321), channel_id=1, source_target_pairs={{0,32},{8,40},{16,48},{24,56},{32,64},{40,72},{48,80},{56,88},{64,... | collective-permute-start | bytes 1544 | tf_op jit(solution)/shard_map/while/body/eval_jaxpr/ppermute | solution.py:20
  823.0 15.2 %collective-permute-start.4 = (f32[128,768]{1,0:T(8,128)}, f32[128,768]{1,0:T(8,128)}, u32[]{:S(2)}, u32[]{:S(2)}) collective-permute-start(f32[128,768]{1,0:T(8,128)} %get-tuple-element.1320), channel_id=1, source_target_pairs={{0,32},{8,40},{16,48},{24,56},{32,64},{40,72},{48,80},{56,88},{64,... | collective-permute-start | bytes 1179656 | tf_op jit(solution)/shard_map/while/body/eval_jaxpr/ppermute | solution.py:20
  823.0 15.2 %collective-permute-start.5 = (f32[128]{0:T(128)S(1)}, f32[128]{0:T(128)S(1)}, u32[]{:S(2)}, u32[]{:S(2)}) collective-permute-start(f32[128]{0:T(128)S(1)} %get-tuple-element.1321), channel_id=1, source_target_pairs={{0,32},{8,40},{16,48},{24,56},{32,64},{40,72},{48,80},{56,88},{64,... | collective-permute-start | bytes 1544 | tf_op jit(solution)/shard_map/while/body/eval_jaxpr/ppermute | solution.py:20
  (5 other events, 9.0 us)
Sparse Core Ops, SparseCore 0:
  16.3 70.3 all-gather.5
where the time goes:
time: 853 us; the launch traced here: 849 us
  waiting for transfers between devices  368 us (43%)
  blocking collectives  156 us (18%)
  starting transfers between devices  109 us (13%)
  matrix products  82.4 us (10%)
  other arithmetic  64.4 us (8%)
  local copies, waits for them, and re-layouts  56.2 us (7%)
  between operations  13.6 us (2%)
    ppermute x42, waiting for transfers between devices, shifted(): return lax.ppermute(value, axis, pairs)  294 us
    all_gather x4, blocking collectives, combined_all(): gathered = jax.tree.map(lambda a: lax.all_gather(a, axis), part)  156 us
    ppermute x42, starting transfers between devices, shifted(): return lax.ppermute(value, axis, pairs)  107 us
    all_gather x1, waiting for transfers between devices, local(): gathered = lax.all_gather(local_rows, 'narrow', axis=0, tiled=True)  68.8 us
    dot_general x16, matrix products, score_block(): lax.dot_general(gathered, center, (((1,), (1,)), ((), ())), preferred_ele...  43.2 us
    dot_general x16, matrix products, block_terms(): lax.dot_general(columns, gathered, (((0,), (0,)), ((), ())), preferred_el...  39.2 us
    while x14, local copies, waits for them, and re-layouts  22.6 us
    reduce_sum x16, other arithmetic, block_terms(): return (numerator, jnp.sum(columns.astype(jnp.float32), axis=0))  19.1 us
  transfers between devices with their start and end apart: 44, of which 30 were waited for; matrix products, arithmetic and copies ran while one was open for 2% of the time, Pallas kernels for 0%

commit v1 on v0

--- a/solution.py
+++ b/solution.py
@@ -52,7 +52,9 @@
     arranged = jnp.take(blocks, block_order, axis=0)
     incoming = from_partner(arranged[half_blocks:], "wide", LEVEL)
     local_rows = jnp.concatenate([arranged[:half_blocks], incoming], axis=0).reshape(-1, feat_width)
-    gathered = lax.all_gather(local_rows, "narrow", axis=0, tiled=True)
+    gathered = jnp.concatenate(
+        lax.all_to_all(jnp.stack([local_rows] * lax.axis_size("narrow")), "narrow", 0, 0), axis=0
+    )
     row_count = gathered.shape[0]
     shard_rows = centers.shape[0]
     score_scale = 4.0 / math.sqrt(feat_width)

time: 853 us -> 817 us (0.958); the launches traced: 849 us -> 802 us
  waiting for transfers between devices: 368 us -> 323 us
  starting transfers between devices: 109 us -> 124 us
  between operations: 13.6 us -> 0.19 us
    all_gather x1 -> x0, waiting for transfers between devices: 68.8 us -> none  [local(): gathered = lax.all_gather(local_rows, 'narrow', axis=0, tiled=True)]
    all_to_all x0 -> x1, waiting for transfers between devices: none -> 36.2 us  [local(): lax.all_to_all(jnp.stack([local_rows] * lax.axis_size('narrow')), 'narrow...]
    ppermute x42, waiting for transfers between devices: 294 us -> 282 us  [shifted(): return lax.ppermute(value, axis, pairs)]
  transfers between devices with their start and end apart: 44 -> 44, of which waited for: 30 -> 30; matrix products, arithmetic and copies ran while one was open for 2% -> 3% of each run, Pallas kernels for 0% -> 0%
where the time goes in v1:
time: 817 us; the launch traced here: 802 us
  waiting for transfers between devices  323 us (40%)
  blocking collectives  151 us (18%)
  starting transfers between devices  124 us (15%)
  matrix products  82.4 us (10%)
  other arithmetic  64.6 us (8%)
  local copies, waits for them, and re-layouts  57.2 us (7%)
    ppermute x42, waiting for transfers between devices, shifted(): return lax.ppermute(value, axis, pairs)  282 us
    all_gather x4, blocking collectives, combined_all(): gathered = jax.tree.map(lambda a: lax.all_gather(a, axis), part)  151 us
    ppermute x42, starting transfers between devices, shifted(): return lax.ppermute(value, axis, pairs)  115 us
    dot_general x16, matrix products, score_block(): lax.dot_general(gathered, center, (((1,), (1,)), ((), ())), preferred_ele...  43.2 us
    dot_general x16, matrix products, block_terms(): lax.dot_general(columns, gathered, (((0,), (0,)), ((), ())), preferred_el...  39.2 us
    all_to_all x1, waiting for transfers between devices, local(): lax.all_to_all(jnp.stack([local_rows] * lax.axis_size('narrow')), 'narrow...  36.2 us
    while x14, local copies, waits for them, and re-layouts  22.6 us
    reduce_sum x16, other arithmetic, block_terms(): return (numerator, jnp.sum(columns.astype(jnp.float32), axis=0))  19.1 us
  transfers between devices with their start and end apart: 44, of which 30 were waited for; matrix products, arithmetic and copies ran while one was open for 3% of the time, Pallas kernels for 0%

profile of v1, /device:TPU:32, one launch (start us, length us, event | category | flops | bytes accessed | tf_op | source)
XLA Modules:
  0.0 802.4 jit_solution(13486877700042134253)
XLA Ops:
  4.0 4.8 collective-permute-done.6
  10.7 6.9 all-to-all-start
  20.3 36.2 %all-to-all-done = bf16[8,256,768]{2,1,0:T(8,128)(2,1)S(1)} async-done(((bf16[8,256,768]{2,1,0:T(8,128)(2,1)}), bf16[8,256,768]{2,1,0:T(8,128)(2,1)S(1)}, u32[]{:S(2)}, u32[]{:S(2)}) %all-to-all-start) | async-done | bytes 3145760 | tf_op jit(solution)/shard_map/all_to_all | solution.py:56
  61.8 124.9 %while.102 = (s32[]{:T(128)}, bf16[128,768]{1,0:T(8,128)(2,1)}, f32[2048,1024]{1,0:T(8,128)}, bf16[2048,768]{1,0:T(8,128)(2,1)S(1)}, s32[]{:T(128)}, /*index=5*/...) while((s32[]{:T(128)}, bf16[128,768]{1,0:T(8,128)(2,1)}, ...), condition=%wide.region_4.5_spmd, body=%wide.region_2.4_spmd.sunk | while | flops 403472416 | bytes 5769536 | solution.py:91
  65.0 11.6 %collective-permute-done = bf16[128,768]{1,0:T(8,128)(2,1)} collective-permute-done((bf16[128,768]{1,0:T(8,128)(2,1)}, bf16[128,768]{1,0:T(8,128)(2,1)}, u32[]{:S(2)}, u32[]{:S(2)}) %collective-permute-start) | collective-permute-done | bytes 196640 | tf_op jit(solution)/shard_map/while/body/eval_jaxpr/ppermute | solution.py:20
  82.6 10.6 %collective-permute-done = bf16[128,768]{1,0:T(8,128)(2,1)} collective-permute-done((bf16[128,768]{1,0:T(8,128)(2,1)}, bf16[128,768]{1,0:T(8,128)(2,1)}, u32[]{:S(2)}, u32[]{:S(2)}) %collective-permute-start) | collective-permute-done | bytes 196640 | tf_op jit(solution)/shard_map/while/body/eval_jaxpr/ppermute | solution.py:20
  100.5 10.3 %collective-permute-done = bf16[128,768]{1,0:T(8,128)(2,1)} collective-permute-done((bf16[128,768]{1,0:T(8,128)(2,1)}, bf16[128,768]{1,0:T(8,128)(2,1)}, u32[]{:S(2)}, u32[]{:S(2)}) %collective-permute-start) | collective-permute-done | bytes 196640 | tf_op jit(solution)/shard_map/while/body/eval_jaxpr/ppermute | solution.py:20
  116.6 11.4 %collective-permute-done = bf16[128,768]{1,0:T(8,128)(2,1)} collective-permute-done((bf16[128,768]{1,0:T(8,128)(2,1)}, bf16[128,768]{1,0:T(8,128)(2,1)}, u32[]{:S(2)}, u32[]{:S(2)}) %collective-permute-start) | collective-permute-done | bytes 196640 | tf_op jit(solution)/shard_map/while/body/eval_jaxpr/ppermute | solution.py:20
  134.5 10.5 %collective-permute-done = bf16[128,768]{1,0:T(8,128)(2,1)} collective-permute-done((bf16[128,768]{1,0:T(8,128)(2,1)}, bf16[128,768]{1,0:T(8,128)(2,1)}, u32[]{:S(2)}, u32[]{:S(2)}) %collective-permute-start) | collective-permute-done | bytes 196640 | tf_op jit(solution)/shard_map/while/body/eval_jaxpr/ppermute | solution.py:20
  150.7 11.5 %collective-permute-done = bf16[128,768]{1,0:T(8,128)(2,1)} collective-permute-done((bf16[128,768]{1,0:T(8,128)(2,1)}, bf16[128,768]{1,0:T(8,128)(2,1)}, u32[]{:S(2)}, u32[]{:S(2)}) %collective-permute-start) | collective-permute-done | bytes 196640 | tf_op jit(solution)/shard_map/while/body/eval_jaxpr/ppermute | solution.py:20
  167.8 13.3 %collective-permute-done = bf16[128,768]{1,0:T(8,128)(2,1)} collective-permute-done((bf16[128,768]{1,0:T(8,128)(2,1)}, bf16[128,768]{1,0:T(8,128)(2,1)}, u32[]{:S(2)}, u32[]{:S(2)}) %collective-permute-start) | collective-permute-done | bytes 196640 | tf_op jit(solution)/shard_map/while/body/eval_jaxpr/ppermute | solution.py:20
  194.9 36.2 %all-gather.1 = f32[16384]{0:T(1024)} all-gather(f32[2048]{0:T(1024)S(1)} %exponential_reduce_fusion.1), channel_id=3, replica_groups=mesh['wide'=32,'narrow'=8] {'narrow'}, dimensions={0}, use_global_device_ids=true | all-gather | bytes 73728 | tf_op jit(solution)/shard_map/all_gather | solution.py:24
  233.3 36.3 %all-gather = f32[16384]{0:T(1024)} all-gather(f32[2048]{0:T(1024)S(1)} %reduce_max.18), channel_id=2, replica_groups=mesh['wide'=32,'narrow'=8] {'narrow'}, dimensions={0}, use_global_device_ids=true | all-gather | bytes 73728 | tf_op jit(solution)/shard_map/all_gather | solution.py:24
  271.8 6.5 while.103
  284.6 142.6 %while.104 = (s32[]{:T(128)}, f32[128,768]{1,0:T(8,128)}, f32[128]{0:T(128)S(1)}, s32[]{:T(128)}, bf16[2048,1024]{1,0:T(8,128)(2,1)}, /*index=5*/bf16[2048,768]{...) while((s32[]{:T(128)}, f32[128,768]{1,0:T(8,128)}, ...), condition=%wide.region_12.13_spmd, body=%wide.region_10.12_spmd.sunk | while | flops 403275808 | bytes 6558088 | solution.py:102
  286.0 16.5 %collective-permute-done.2 = f32[128]{0:T(128)S(1)} collective-permute-done((f32[128]{0:T(128)S(1)}, f32[128]{0:T(128)S(1)}, u32[]{:S(2)}, u32[]{:S(2)}) %collective-permute-start.2) | collective-permute-done | bytes 544 | tf_op jit(solution)/shard_map/while/body/eval_jaxpr/ppermute | solution.py:20
  308.5 12.3 %collective-permute-done.2 = f32[128]{0:T(128)S(1)} collective-permute-done((f32[128]{0:T(128)S(1)}, f32[128]{0:T(128)S(1)}, u32[]{:S(2)}, u32[]{:S(2)}) %collective-permute-start.2) | collective-permute-done | bytes 544 | tf_op jit(solution)/shard_map/while/body/eval_jaxpr/ppermute | solution.py:20
  329.1 11.1 %collective-permute-done.2 = f32[128]{0:T(128)S(1)} collective-permute-done((f32[128]{0:T(128)S(1)}, f32[128]{0:T(128)S(1)}, u32[]{:S(2)}, u32[]{:S(2)}) %collective-permute-start.2) | collective-permute-done | bytes 544 | tf_op jit(solution)/shard_map/while/body/eval_jaxpr/ppermute | solution.py:20
  345.5 18.9 %collective-permute-done.2 = f32[128]{0:T(128)S(1)} collective-permute-done((f32[128]{0:T(128)S(1)}, f32[128]{0:T(128)S(1)}, u32[]{:S(2)}, u32[]{:S(2)}) %collective-permute-start.2) | collective-permute-done | bytes 544 | tf_op jit(solution)/shard_map/while/body/eval_jaxpr/ppermute | solution.py:20
  367.0 6.6 collective-permute-start.2
  375.0 13.6 %collective-permute-done.2 = f32[128]{0:T(128)S(1)} collective-permute-done((f32[128]{0:T(128)S(1)}, f32[128]{0:T(128)S(1)}, u32[]{:S(2)}, u32[]{:S(2)}) %collective-permute-start.2) | collective-permute-done | bytes 544 | tf_op jit(solution)/shard_map/while/body/eval_jaxpr/ppermute | solution.py:20
  391.2 5.9 collective-permute-start.2
  398.4 11.7 %collective-permute-done.2 = f32[128]{0:T(128)S(1)} collective-permute-done((f32[128]{0:T(128)S(1)}, f32[128]{0:T(128)S(1)}, u32[]{:S(2)}, u32[]{:S(2)}) %collective-permute-start.2) | collective-permute-done | bytes 544 | tf_op jit(solution)/shard_map/while/body/eval_jaxpr/ppermute | solution.py:20
  415.5 9.1 %collective-permute-done.2 = f32[128]{0:T(128)S(1)} collective-permute-done((f32[128]{0:T(128)S(1)}, f32[128]{0:T(128)S(1)}, u32[]{:S(2)}, u32[]{:S(2)}) %collective-permute-start.2) | collective-permute-done | bytes 544 | tf_op jit(solution)/shard_map/while/body/eval_jaxpr/ppermute | solution.py:20
  434.5 121.3 %while.105 = (s32[]{:T(128)}, bf16[128,768]{1,0:T(8,128)(2,1)}, f32[2048,1024]{1,0:T(8,128)}, bf16[2048,768]{1,0:T(8,128)(2,1)S(1)}, s32[]{:T(128)}, /*index=5*/...) while((s32[]{:T(128)}, bf16[128,768]{1,0:T(8,128)(2,1)}, ...), condition=%wide.region_16.17_spmd, body=%wide.region_14.16_spmd.sunk | while | flops 403472416 | bytes 5769536 | solution.py:91
  436.0 12.2 %collective-permute-done.3 = bf16[128,768]{1,0:T(8,128)(2,1)} collective-permute-done((bf16[128,768]{1,0:T(8,128)(2,1)}, bf16[128,768]{1,0:T(8,128)(2,1)}, u32[]{:S(2)}, u32[]{:S(2)}) %collective-permute-start.3) | collective-permute-done | bytes 196640 | tf_op jit(solution)/shard_map/while/body/eval_jaxpr/ppermute | solution.py:20
  455.8 10.8 %collective-permute-done.3 = bf16[128,768]{1,0:T(8,128)(2,1)} collective-permute-done((bf16[128,768]{1,0:T(8,128)(2,1)}, bf16[128,768]{1,0:T(8,128)(2,1)}, u32[]{:S(2)}, u32[]{:S(2)}) %collective-permute-start.3) | collective-permute-done | bytes 196640 | tf_op jit(solution)/shard_map/while/body/eval_jaxpr/ppermute | solution.py:20
  474.6 8.7 %collective-permute-done.3 = bf16[128,768]{1,0:T(8,128)(2,1)} collective-permute-done((bf16[128,768]{1,0:T(8,128)(2,1)}, bf16[128,768]{1,0:T(8,128)(2,1)}, u32[]{:S(2)}, u32[]{:S(2)}) %collective-permute-start.3) | collective-permute-done | bytes 196640 | tf_op jit(solution)/shard_map/while/body/eval_jaxpr/ppermute | solution.py:20
  488.9 5.8 collective-permute-start.3
  509.8 4.9 collective-permute-done.3
  520.3 8.3 %collective-permute-start.3 = (bf16[128,768]{1,0:T(8,128)(2,1)}, bf16[128,768]{1,0:T(8,128)(2,1)}, u32[]{:S(2)}, u32[]{:S(2)}) collective-permute-start(bf16[128,768]{1,0:T(8,128)(2,1)} %get-tuple-element.1261), channel_id=1, source_target_pairs={{0,32},{8,40},{16,48},{24,56},{32,64},{40,72},{48,80},{56,88},{64,... | collective-permute-start | bytes 589832 | tf_op jit(solution)/shard_map/while/body/eval_jaxpr/ppermute | solution.py:20
  528.6 5.3 collective-permute-done.3
  539.5 7.1 collective-permute-start.3
  564.0 41.6 %all-gather.3 = f32[16384]{0:T(1024)} all-gather(f32[2048]{0:T(1024)S(1)} %exponential_reduce_fusion), channel_id=5, replica_groups=mesh['wide'=32,'narrow'=8] {'narrow'}, dimensions={0}, use_global_device_ids=true | all-gather | bytes 73728 | tf_op jit(solution)/shard_map/all_gather | solution.py:24
  607.8 36.5 %all-gather.2 = f32[16384]{0:T(1024)} all-gather(f32[2048]{0:T(1024)S(1)} %reduce_max.19), channel_id=4, replica_groups=mesh['wide'=32,'narrow'=8] {'narrow'}, dimensions={0}, use_global_device_ids=true | all-gather | bytes 73728 | tf_op jit(solution)/shard_map/all_gather | solution.py:24
  646.5 6.5 while.106
  659.3 141.2 %while.107 = (s32[]{:T(128)}, f32[128,768]{1,0:T(8,128)}, f32[128]{0:T(128)S(1)}, s32[]{:T(128)}, bf16[2048,1024]{1,0:T(8,128)(2,1)}, /*index=5*/bf16[2048,768]{...) while((s32[]{:T(128)}, f32[128,768]{1,0:T(8,128)}, ...), condition=%wide.region_24.25_spmd, body=%wide.region_22.24_spmd.sunk | while | flops 403275808 | bytes 6558088 | solution.py:102
  659.3 6.0 collective-permute-start.5
  666.6 8.6 %collective-permute-done.5 = f32[128]{0:T(128)S(1)} collective-permute-done((f32[128]{0:T(128)S(1)}, f32[128]{0:T(128)S(1)}, u32[]{:S(2)}, u32[]{:S(2)}) %collective-permute-start.5) | collective-permute-done | bytes 544 | tf_op jit(solution)/shard_map/while/body/eval_jaxpr/ppermute | solution.py:20
  677.8 10.0 %collective-permute-start.5 = (f32[128]{0:T(128)S(1)}, f32[128]{0:T(128)S(1)}, u32[]{:S(2)}, u32[]{:S(2)}) collective-permute-start(f32[128]{0:T(128)S(1)} %get-tuple-element.1321), channel_id=1, source_target_pairs={{0,32},{8,40},{16,48},{24,56},{32,64},{40,72},{48,80},{56,88},{64,... | collective-permute-start | bytes 1544 | tf_op jit(solution)/shard_map/while/body/eval_jaxpr/ppermute | solution.py:20
  689.1 10.5 %collective-permute-done.5 = f32[128]{0:T(128)S(1)} collective-permute-done((f32[128]{0:T(128)S(1)}, f32[128]{0:T(128)S(1)}, u32[]{:S(2)}, u32[]{:S(2)}) %collective-permute-start.5) | collective-permute-done | bytes 544 | tf_op jit(solution)/shard_map/while/body/eval_jaxpr/ppermute | solution.py:20
  702.1 7.2 collective-permute-start.5
  710.6 7.1 collective-permute-done.5
  723.0 12.6 %collective-permute-start.5 = (f32[128]{0:T(128)S(1)}, f32[128]{0:T(128)S(1)}, u32[]{:S(2)}, u32[]{:S(2)}) collective-permute-start(f32[128]{0:T(128)S(1)} %get-tuple-element.1321), channel_id=1, source_target_pairs={{0,32},{8,40},{16,48},{24,56},{32,64},{40,72},{48,80},{56,88},{64,... | collective-permute-start | bytes 1544 | tf_op jit(solution)/shard_map/while/body/eval_jaxpr/ppermute | solution.py:20
  737.0 9.5 %collective-permute-done.5 = f32[128]{0:T(128)S(1)} collective-permute-done((f32[128]{0:T(128)S(1)}, f32[128]{0:T(128)S(1)}, u32[]{:S(2)}, u32[]{:S(2)}) %collective-permute-start.5) | collective-permute-done | bytes 544 | tf_op jit(solution)/shard_map/while/body/eval_jaxpr/ppermute | solution.py:20
  759.2 5.3 collective-permute-done.5
  774.3 10.0 %collective-permute-done.5 = f32[128]{0:T(128)S(1)} collective-permute-done((f32[128]{0:T(128)S(1)}, f32[128]{0:T(128)S(1)}, u32[]{:S(2)}, u32[]{:S(2)}) %collective-permute-start.5) | collective-permute-done | bytes 544 | tf_op jit(solution)/shard_map/while/body/eval_jaxpr/ppermute | solution.py:20
  789.2 8.8 %collective-permute-done.5 = f32[128]{0:T(128)S(1)} collective-permute-done((f32[128]{0:T(128)S(1)}, f32[128]{0:T(128)S(1)}, u32[]{:S(2)}, u32[]{:S(2)}) %collective-permute-start.5) | collective-permute-done | bytes 544 | tf_op jit(solution)/shard_map/while/body/eval_jaxpr/ppermute | solution.py:20
  (232 shorter events, 259.8 us)
Async XLA Ops:
  2.1 6.7 collective-permute-start.6
  10.7 45.8 %all-to-all-start = ((bf16[8,256,768]{2,1,0:T(8,128)(2,1)}), bf16[8,256,768]{2,1,0:T(8,128)(2,1)S(1)}, u32[]{:S(2)}, u32[]{:S(2)}) async-start(bf16[8,256,768]{2,1,0:T(8,128)(2,1)} %stack.3), calls=%async_computation | async-start | bytes 6291456 | tf_op jit(solution)/shard_map/all_to_all | solution.py:56
  58.5 3.2 copy-start.2
  61.8 14.8 %collective-permute-start = (bf16[128,768]{1,0:T(8,128)(2,1)}, bf16[128,768]{1,0:T(8,128)(2,1)}, u32[]{:S(2)}, u32[]{:S(2)}) collective-permute-start(bf16[128,768]{1,0:T(8,128)(2,1)} %get-tuple-element.1165), channel_id=1, source_target_pairs={{0,32},{8,40},{16,48},{24,56},{32,64},{40,72},{48,80},{56,88},{64,... | collective-permute-start | bytes 589832 | tf_op jit(solution)/shard_map/while/body/eval_jaxpr/ppermute | solution.py:20
  82.2 11.0 %collective-permute-start = (bf16[128,768]{1,0:T(8,128)(2,1)}, bf16[128,768]{1,0:T(8,128)(2,1)}, u32[]{:S(2)}, u32[]{:S(2)}) collective-permute-start(bf16[128,768]{1,0:T(8,128)(2,1)} %get-tuple-element.1165), channel_id=1, source_target_pairs={{0,32},{8,40},{16,48},{24,56},{32,64},{40,72},{48,80},{56,88},{64,... | collective-permute-start | bytes 589832 | tf_op jit(solution)/shard_map/while/body/eval_jaxpr/ppermute | solution.py:20
  98.8 12.0 %collective-permute-start = (bf16[128,768]{1,0:T(8,128)(2,1)}, bf16[128,768]{1,0:T(8,128)(2,1)}, u32[]{:S(2)}, u32[]{:S(2)}) collective-permute-start(bf16[128,768]{1,0:T(8,128)(2,1)} %get-tuple-element.1165), channel_id=1, source_target_pairs={{0,32},{8,40},{16,48},{24,56},{32,64},{40,72},{48,80},{56,88},{64,... | collective-permute-start | bytes 589832 | tf_op jit(solution)/shard_map/while/body/eval_jaxpr/ppermute | solution.py:20
  116.5 11.5 %collective-permute-start = (bf16[128,768]{1,0:T(8,128)(2,1)}, bf16[128,768]{1,0:T(8,128)(2,1)}, u32[]{:S(2)}, u32[]{:S(2)}) collective-permute-start(bf16[128,768]{1,0:T(8,128)(2,1)} %get-tuple-element.1165), channel_id=1, source_target_pairs={{0,32},{8,40},{16,48},{24,56},{32,64},{40,72},{48,80},{56,88},{64,... | collective-permute-start | bytes 589832 | tf_op jit(solution)/shard_map/while/body/eval_jaxpr/ppermute | solution.py:20
  133.5 11.5 %collective-permute-start = (bf16[128,768]{1,0:T(8,128)(2,1)}, bf16[128,768]{1,0:T(8,128)(2,1)}, u32[]{:S(2)}, u32[]{:S(2)}) collective-permute-start(bf16[128,768]{1,0:T(8,128)(2,1)} %get-tuple-element.1165), channel_id=1, source_target_pairs={{0,32},{8,40},{16,48},{24,56},{32,64},{40,72},{48,80},{56,88},{64,... | collective-permute-start | bytes 589832 | tf_op jit(solution)/shard_map/while/body/eval_jaxpr/ppermute | solution.py:20
  150.7 11.5 %collective-permute-start = (bf16[128,768]{1,0:T(8,128)(2,1)}, bf16[128,768]{1,0:T(8,128)(2,1)}, u32[]{:S(2)}, u32[]{:S(2)}) collective-permute-start(bf16[128,768]{1,0:T(8,128)(2,1)} %get-tuple-element.1165), channel_id=1, source_target_pairs={{0,32},{8,40},{16,48},{24,56},{32,64},{40,72},{48,80},{56,88},{64,... | collective-permute-start | bytes 589832 | tf_op jit(solution)/shard_map/while/body/eval_jaxpr/ppermute | solution.py:20
  167.8 13.3 %collective-permute-start = (bf16[128,768]{1,0:T(8,128)(2,1)}, bf16[128,768]{1,0:T(8,128)(2,1)}, u32[]{:S(2)}, u32[]{:S(2)}) collective-permute-start(bf16[128,768]{1,0:T(8,128)(2,1)} %get-tuple-element.1165), channel_id=1, source_target_pairs={{0,32},{8,40},{16,48},{24,56},{32,64},{40,72},{48,80},{56,88},{64,... | collective-permute-start | bytes 589832 | tf_op jit(solution)/shard_map/while/body/eval_jaxpr/ppermute | solution.py:20
  282.5 2.1 copy-start.4
  284.6 17.9 %collective-permute-start.1 = (f32[128,768]{1,0:T(8,128)}, f32[128,768]{1,0:T(8,128)}, u32[]{:S(2)}, u32[]{:S(2)}) collective-permute-start(f32[128,768]{1,0:T(8,128)} %get-tuple-element.1224), channel_id=1, source_target_pairs={{0,32},{8,40},{16,48},{24,56},{32,64},{40,72},{48,80},{56,88},{64,... | collective-permute-start | bytes 1179656 | tf_op jit(solution)/shard_map/while/body/eval_jaxpr/ppermute | solution.py:20
  284.6 17.9 %collective-permute-start.2 = (f32[128]{0:T(128)S(1)}, f32[128]{0:T(128)S(1)}, u32[]{:S(2)}, u32[]{:S(2)}) collective-permute-start(f32[128]{0:T(128)S(1)} %get-tuple-element.1225), channel_id=1, source_target_pairs={{0,32},{8,40},{16,48},{24,56},{32,64},{40,72},{48,80},{56,88},{64,... | collective-permute-start | bytes 1544 | tf_op jit(solution)/shard_map/while/body/eval_jaxpr/ppermute | solution.py:20
  305.1 15.8 %collective-permute-start.1 = (f32[128,768]{1,0:T(8,128)}, f32[128,768]{1,0:T(8,128)}, u32[]{:S(2)}, u32[]{:S(2)}) collective-permute-start(f32[128,768]{1,0:T(8,128)} %get-tuple-element.1224), channel_id=1, source_target_pairs={{0,32},{8,40},{16,48},{24,56},{32,64},{40,72},{48,80},{56,88},{64,... | collective-permute-start | bytes 1179656 | tf_op jit(solution)/shard_map/while/body/eval_jaxpr/ppermute | solution.py:20
  307.2 13.7 %collective-permute-start.2 = (f32[128]{0:T(128)S(1)}, f32[128]{0:T(128)S(1)}, u32[]{:S(2)}, u32[]{:S(2)}) collective-permute-start(f32[128]{0:T(128)S(1)} %get-tuple-element.1225), channel_id=1, source_target_pairs={{0,32},{8,40},{16,48},{24,56},{32,64},{40,72},{48,80},{56,88},{64,... | collective-permute-start | bytes 1544 | tf_op jit(solution)/shard_map/while/body/eval_jaxpr/ppermute | solution.py:20
  323.4 16.8 %collective-permute-start.1 = (f32[128,768]{1,0:T(8,128)}, f32[128,768]{1,0:T(8,128)}, u32[]{:S(2)}, u32[]{:S(2)}) collective-permute-start(f32[128,768]{1,0:T(8,128)} %get-tuple-element.1224), channel_id=1, source_target_pairs={{0,32},{8,40},{16,48},{24,56},{32,64},{40,72},{48,80},{56,88},{64,... | collective-permute-start | bytes 1179656 | tf_op jit(solution)/shard_map/while/body/eval_jaxpr/ppermute | solution.py:20
  326.8 13.4 %collective-permute-start.2 = (f32[128]{0:T(128)S(1)}, f32[128]{0:T(128)S(1)}, u32[]{:S(2)}, u32[]{:S(2)}) collective-permute-start(f32[128]{0:T(128)S(1)} %get-tuple-element.1225), channel_id=1, source_target_pairs={{0,32},{8,40},{16,48},{24,56},{32,64},{40,72},{48,80},{56,88},{64,... | collective-permute-start | bytes 1544 | tf_op jit(solution)/shard_map/while/body/eval_jaxpr/ppermute | solution.py:20
  342.7 21.7 %collective-permute-start.1 = (f32[128,768]{1,0:T(8,128)}, f32[128,768]{1,0:T(8,128)}, u32[]{:S(2)}, u32[]{:S(2)}) collective-permute-start(f32[128,768]{1,0:T(8,128)} %get-tuple-element.1224), channel_id=1, source_target_pairs={{0,32},{8,40},{16,48},{24,56},{32,64},{40,72},{48,80},{56,88},{64,... | collective-permute-start | bytes 1179656 | tf_op jit(solution)/shard_map/while/body/eval_jaxpr/ppermute | solution.py:20
  342.7 21.7 %collective-permute-start.2 = (f32[128]{0:T(128)S(1)}, f32[128]{0:T(128)S(1)}, u32[]{:S(2)}, u32[]{:S(2)}) collective-permute-start(f32[128]{0:T(128)S(1)} %get-tuple-element.1225), channel_id=1, source_target_pairs={{0,32},{8,40},{16,48},{24,56},{32,64},{40,72},{48,80},{56,88},{64,... | collective-permute-start | bytes 1544 | tf_op jit(solution)/shard_map/while/body/eval_jaxpr/ppermute | solution.py:20
  367.0 21.6 %collective-permute-start.1 = (f32[128,768]{1,0:T(8,128)}, f32[128,768]{1,0:T(8,128)}, u32[]{:S(2)}, u32[]{:S(2)}) collective-permute-start(f32[128,768]{1,0:T(8,128)} %get-tuple-element.1224), channel_id=1, source_target_pairs={{0,32},{8,40},{16,48},{24,56},{32,64},{40,72},{48,80},{56,88},{64,... | collective-permute-start | bytes 1179656 | tf_op jit(solution)/shard_map/while/body/eval_jaxpr/ppermute | solution.py:20
  367.0 21.6 %collective-permute-start.2 = (f32[128]{0:T(128)S(1)}, f32[128]{0:T(128)S(1)}, u32[]{:S(2)}, u32[]{:S(2)}) collective-permute-start(f32[128]{0:T(128)S(1)} %get-tuple-element.1225), channel_id=1, source_target_pairs={{0,32},{8,40},{16,48},{24,56},{32,64},{40,72},{48,80},{56,88},{64,... | collective-permute-start | bytes 1544 | tf_op jit(solution)/shard_map/while/body/eval_jaxpr/ppermute | solution.py:20
  391.2 18.9 %collective-permute-start.1 = (f32[128,768]{1,0:T(8,128)}, f32[128,768]{1,0:T(8,128)}, u32[]{:S(2)}, u32[]{:S(2)}) collective-permute-start(f32[128,768]{1,0:T(8,128)} %get-tuple-element.1224), channel_id=1, source_target_pairs={{0,32},{8,40},{16,48},{24,56},{32,64},{40,72},{48,80},{56,88},{64,... | collective-permute-start | bytes 1179656 | tf_op jit(solution)/shard_map/while/body/eval_jaxpr/ppermute | solution.py:20
  391.2 18.9 %collective-permute-start.2 = (f32[128]{0:T(128)S(1)}, f32[128]{0:T(128)S(1)}, u32[]{:S(2)}, u32[]{:S(2)}) collective-permute-start(f32[128]{0:T(128)S(1)} %get-tuple-element.1225), channel_id=1, source_target_pairs={{0,32},{8,40},{16,48},{24,56},{32,64},{40,72},{48,80},{56,88},{64,... | collective-permute-start | bytes 1544 | tf_op jit(solution)/shard_map/while/body/eval_jaxpr/ppermute | solution.py:20
  412.6 12.0 %collective-permute-start.1 = (f32[128,768]{1,0:T(8,128)}, f32[128,768]{1,0:T(8,128)}, u32[]{:S(2)}, u32[]{:S(2)}) collective-permute-start(f32[128,768]{1,0:T(8,128)} %get-tuple-element.1224), channel_id=1, source_target_pairs={{0,32},{8,40},{16,48},{24,56},{32,64},{40,72},{48,80},{56,88},{64,... | collective-permute-start | bytes 1179656 | tf_op jit(solution)/shard_map/while/body/eval_jaxpr/ppermute | solution.py:20
  412.7 12.0 %collective-permute-start.2 = (f32[128]{0:T(128)S(1)}, f32[128]{0:T(128)S(1)}, u32[]{:S(2)}, u32[]{:S(2)}) collective-permute-start(f32[128]{0:T(128)S(1)} %get-tuple-element.1225), channel_id=1, source_target_pairs={{0,32},{8,40},{16,48},{24,56},{32,64},{40,72},{48,80},{56,88},{64,... | collective-permute-start | bytes 1544 | tf_op jit(solution)/shard_map/while/body/eval_jaxpr/ppermute | solution.py:20
  431.2 3.2 copy-start.1
  434.5 13.8 %collective-permute-start.3 = (bf16[128,768]{1,0:T(8,128)(2,1)}, bf16[128,768]{1,0:T(8,128)(2,1)}, u32[]{:S(2)}, u32[]{:S(2)}) collective-permute-start(bf16[128,768]{1,0:T(8,128)(2,1)} %get-tuple-element.1261), channel_id=1, source_target_pairs={{0,32},{8,40},{16,48},{24,56},{32,64},{40,72},{48,80},{56,88},{64,... | collective-permute-start | bytes 589832 | tf_op jit(solution)/shard_map/while/body/eval_jaxpr/ppermute | solution.py:20
  453.8 12.8 %collective-permute-start.3 = (bf16[128,768]{1,0:T(8,128)(2,1)}, bf16[128,768]{1,0:T(8,128)(2,1)}, u32[]{:S(2)}, u32[]{:S(2)}) collective-permute-start(bf16[128,768]{1,0:T(8,128)(2,1)} %get-tuple-element.1261), channel_id=1, source_target_pairs={{0,32},{8,40},{16,48},{24,56},{32,64},{40,72},{48,80},{56,88},{64,... | collective-permute-start | bytes 589832 | tf_op jit(solution)/shard_map/while/body/eval_jaxpr/ppermute | solution.py:20
  472.2 11.1 %collective-permute-start.3 = (bf16[128,768]{1,0:T(8,128)(2,1)}, bf16[128,768]{1,0:T(8,128)(2,1)}, u32[]{:S(2)}, u32[]{:S(2)}) collective-permute-start(bf16[128,768]{1,0:T(8,128)(2,1)} %get-tuple-element.1261), channel_id=1, source_target_pairs={{0,32},{8,40},{16,48},{24,56},{32,64},{40,72},{48,80},{56,88},{64,... | collective-permute-start | bytes 589832 | tf_op jit(solution)/shard_map/while/body/eval_jaxpr/ppermute | solution.py:20
  488.9 10.5 %collective-permute-start.3 = (bf16[128,768]{1,0:T(8,128)(2,1)}, bf16[128,768]{1,0:T(8,128)(2,1)}, u32[]{:S(2)}, u32[]{:S(2)}) collective-permute-start(bf16[128,768]{1,0:T(8,128)(2,1)} %get-tuple-element.1261), channel_id=1, source_target_pairs={{0,32},{8,40},{16,48},{24,56},{32,64},{40,72},{48,80},{56,88},{64,... | collective-permute-start | bytes 589832 | tf_op jit(solution)/shard_map/while/body/eval_jaxpr/ppermute | solution.py:20
  505.1 9.6 %collective-permute-start.3 = (bf16[128,768]{1,0:T(8,128)(2,1)}, bf16[128,768]{1,0:T(8,128)(2,1)}, u32[]{:S(2)}, u32[]{:S(2)}) collective-permute-start(bf16[128,768]{1,0:T(8,128)(2,1)} %get-tuple-element.1261), channel_id=1, source_target_pairs={{0,32},{8,40},{16,48},{24,56},{32,64},{40,72},{48,80},{56,88},{64,... | collective-permute-start | bytes 589832 | tf_op jit(solution)/shard_map/while/body/eval_jaxpr/ppermute | solution.py:20
  520.3 13.6 %collective-permute-start.3 = (bf16[128,768]{1,0:T(8,128)(2,1)}, bf16[128,768]{1,0:T(8,128)(2,1)}, u32[]{:S(2)}, u32[]{:S(2)}) collective-permute-start(bf16[128,768]{1,0:T(8,128)(2,1)} %get-tuple-element.1261), channel_id=1, source_target_pairs={{0,32},{8,40},{16,48},{24,56},{32,64},{40,72},{48,80},{56,88},{64,... | collective-permute-start | bytes 589832 | tf_op jit(solution)/shard_map/while/body/eval_jaxpr/ppermute | solution.py:20
  539.5 10.6 %collective-permute-start.3 = (bf16[128,768]{1,0:T(8,128)(2,1)}, bf16[128,768]{1,0:T(8,128)(2,1)}, u32[]{:S(2)}, u32[]{:S(2)}) collective-permute-start(bf16[128,768]{1,0:T(8,128)(2,1)} %get-tuple-element.1261), channel_id=1, source_target_pairs={{0,32},{8,40},{16,48},{24,56},{32,64},{40,72},{48,80},{56,88},{64,... | collective-permute-start | bytes 589832 | tf_op jit(solution)/shard_map/while/body/eval_jaxpr/ppermute | solution.py:20
  657.2 2.1 copy-start.3
  659.3 15.9 %collective-permute-start.4 = (f32[128,768]{1,0:T(8,128)}, f32[128,768]{1,0:T(8,128)}, u32[]{:S(2)}, u32[]{:S(2)}) collective-permute-start(f32[128,768]{1,0:T(8,128)} %get-tuple-element.1320), channel_id=1, source_target_pairs={{0,32},{8,40},{16,48},{24,56},{32,64},{40,72},{48,80},{56,88},{64,... | collective-permute-start | bytes 1179656 | tf_op jit(solution)/shard_map/while/body/eval_jaxpr/ppermute | solution.py:20
  659.3 15.9 %collective-permute-start.5 = (f32[128]{0:T(128)S(1)}, f32[128]{0:T(128)S(1)}, u32[]{:S(2)}, u32[]{:S(2)}) collective-permute-start(f32[128]{0:T(128)S(1)} %get-tuple-element.1321), channel_id=1, source_target_pairs={{0,32},{8,40},{16,48},{24,56},{32,64},{40,72},{48,80},{56,88},{64,... | collective-permute-start | bytes 1544 | tf_op jit(solution)/shard_map/while/body/eval_jaxpr/ppermute | solution.py:20
  677.8 21.8 %collective-permute-start.4 = (f32[128,768]{1,0:T(8,128)}, f32[128,768]{1,0:T(8,128)}, u32[]{:S(2)}, u32[]{:S(2)}) collective-permute-start(f32[128,768]{1,0:T(8,128)} %get-tuple-element.1320), channel_id=1, source_target_pairs={{0,32},{8,40},{16,48},{24,56},{32,64},{40,72},{48,80},{56,88},{64,... | collective-permute-start | bytes 1179656 | tf_op jit(solution)/shard_map/while/body/eval_jaxpr/ppermute | solution.py:20
  677.8 21.7 %collective-permute-start.5 = (f32[128]{0:T(128)S(1)}, f32[128]{0:T(128)S(1)}, u32[]{:S(2)}, u32[]{:S(2)}) collective-permute-start(f32[128]{0:T(128)S(1)} %get-tuple-element.1321), channel_id=1, source_target_pairs={{0,32},{8,40},{16,48},{24,56},{32,64},{40,72},{48,80},{56,88},{64,... | collective-permute-start | bytes 1544 | tf_op jit(solution)/shard_map/while/body/eval_jaxpr/ppermute | solution.py:20
  702.1 15.6 %collective-permute-start.4 = (f32[128,768]{1,0:T(8,128)}, f32[128,768]{1,0:T(8,128)}, u32[]{:S(2)}, u32[]{:S(2)}) collective-permute-start(f32[128,768]{1,0:T(8,128)} %get-tuple-element.1320), channel_id=1, source_target_pairs={{0,32},{8,40},{16,48},{24,56},{32,64},{40,72},{48,80},{56,88},{64,... | collective-permute-start | bytes 1179656 | tf_op jit(solution)/shard_map/while/body/eval_jaxpr/ppermute | solution.py:20
  702.1 15.6 %collective-permute-start.5 = (f32[128]{0:T(128)S(1)}, f32[128]{0:T(128)S(1)}, u32[]{:S(2)}, u32[]{:S(2)}) collective-permute-start(f32[128]{0:T(128)S(1)} %get-tuple-element.1321), channel_id=1, source_target_pairs={{0,32},{8,40},{16,48},{24,56},{32,64},{40,72},{48,80},{56,88},{64,... | collective-permute-start | bytes 1544 | tf_op jit(solution)/shard_map/while/body/eval_jaxpr/ppermute | solution.py:20
  720.3 26.2 %collective-permute-start.4 = (f32[128,768]{1,0:T(8,128)}, f32[128,768]{1,0:T(8,128)}, u32[]{:S(2)}, u32[]{:S(2)}) collective-permute-start(f32[128,768]{1,0:T(8,128)} %get-tuple-element.1320), channel_id=1, source_target_pairs={{0,32},{8,40},{16,48},{24,56},{32,64},{40,72},{48,80},{56,88},{64,... | collective-permute-start | bytes 1179656 | tf_op jit(solution)/shard_map/while/body/eval_jaxpr/ppermute | solution.py:20
  723.0 23.4 %collective-permute-start.5 = (f32[128]{0:T(128)S(1)}, f32[128]{0:T(128)S(1)}, u32[]{:S(2)}, u32[]{:S(2)}) collective-permute-start(f32[128]{0:T(128)S(1)} %get-tuple-element.1321), channel_id=1, source_target_pairs={{0,32},{8,40},{16,48},{24,56},{32,64},{40,72},{48,80},{56,88},{64,... | collective-permute-start | bytes 1544 | tf_op jit(solution)/shard_map/while/body/eval_jaxpr/ppermute | solution.py:20
  749.0 15.4 %collective-permute-start.4 = (f32[128,768]{1,0:T(8,128)}, f32[128,768]{1,0:T(8,128)}, u32[]{:S(2)}, u32[]{:S(2)}) collective-permute-start(f32[128,768]{1,0:T(8,128)} %get-tuple-element.1320), channel_id=1, source_target_pairs={{0,32},{8,40},{16,48},{24,56},{32,64},{40,72},{48,80},{56,88},{64,... | collective-permute-start | bytes 1179656 | tf_op jit(solution)/shard_map/while/body/eval_jaxpr/ppermute | solution.py:20
  753.2 11.2 %collective-permute-start.5 = (f32[128]{0:T(128)S(1)}, f32[128]{0:T(128)S(1)}, u32[]{:S(2)}, u32[]{:S(2)}) collective-permute-start(f32[128]{0:T(128)S(1)} %get-tuple-element.1321), channel_id=1, source_target_pairs={{0,32},{8,40},{16,48},{24,56},{32,64},{40,72},{48,80},{56,88},{64,... | collective-permute-start | bytes 1544 | tf_op jit(solution)/shard_map/while/body/eval_jaxpr/ppermute | solution.py:20
  767.0 17.3 %collective-permute-start.4 = (f32[128,768]{1,0:T(8,128)}, f32[128,768]{1,0:T(8,128)}, u32[]{:S(2)}, u32[]{:S(2)}) collective-permute-start(f32[128,768]{1,0:T(8,128)} %get-tuple-element.1320), channel_id=1, source_target_pairs={{0,32},{8,40},{16,48},{24,56},{32,64},{40,72},{48,80},{56,88},{64,... | collective-permute-start | bytes 1179656 | tf_op jit(solution)/shard_map/while/body/eval_jaxpr/ppermute | solution.py:20
  769.2 15.0 %collective-permute-start.5 = (f32[128]{0:T(128)S(1)}, f32[128]{0:T(128)S(1)}, u32[]{:S(2)}, u32[]{:S(2)}) collective-permute-start(f32[128]{0:T(128)S(1)} %get-tuple-element.1321), channel_id=1, source_target_pairs={{0,32},{8,40},{16,48},{24,56},{32,64},{40,72},{48,80},{56,88},{64,... | collective-permute-start | bytes 1544 | tf_op jit(solution)/shard_map/while/body/eval_jaxpr/ppermute | solution.py:20
  786.8 11.2 %collective-permute-start.4 = (f32[128,768]{1,0:T(8,128)}, f32[128,768]{1,0:T(8,128)}, u32[]{:S(2)}, u32[]{:S(2)}) collective-permute-start(f32[128,768]{1,0:T(8,128)} %get-tuple-element.1320), channel_id=1, source_target_pairs={{0,32},{8,40},{16,48},{24,56},{32,64},{40,72},{48,80},{56,88},{64,... | collective-permute-start | bytes 1179656 | tf_op jit(solution)/shard_map/while/body/eval_jaxpr/ppermute | solution.py:20
  786.8 11.2 %collective-permute-start.5 = (f32[128]{0:T(128)S(1)}, f32[128]{0:T(128)S(1)}, u32[]{:S(2)}, u32[]{:S(2)}) collective-permute-start(f32[128]{0:T(128)S(1)} %get-tuple-element.1321), channel_id=1, source_target_pairs={{0,32},{8,40},{16,48},{24,56},{32,64},{40,72},{48,80},{56,88},{64,... | collective-permute-start | bytes 1544 | tf_op jit(solution)/shard_map/while/body/eval_jaxpr/ppermute | solution.py:20
  (3 other events, 4.2 us)
